TPU v7x, 512 devices: a whole 4x4x16 slice. The times are simulated.
512 devices in a mesh: req: 32 (over z, core), hid: 16 (over x, y).
Axes of the slice: x: 4, y: 4, z: 16, core: 2. Of those that a mesh axis runs over, the one named last changes fastest.
Arguments:
- attn_partial: bfloat16 [16, 2048, 2880], P('hid', 'req'), may hold values from -4 to 4
- residual: bfloat16 [2048, 2880], P('req'), may hold values from -6 to 6
- norm_gain: bfloat16 [2880], replicated, may hold values from 0.5 to 1.5
- router_weight: bfloat16 [2880, 32], replicated, may hold values from -0.02734375 to 0.02734375
- router_bias: float32 [32], replicated, may hold values from -2.5 to 2.5
- routes: int32 [2048, 4], P('req'), may hold values from 0 to 31, all different within a row; in each aligned block of 64 rows (0 to 63, 64 to 127, ...) at most 16 rows name the same one
- gate_up: bfloat16 [32, 2880, 5760], P('req', None, 'hid'), may hold values from -0.109375 to 0.109375
- gate_up_bias: bfloat16 [32, 5760], P('req', 'hid'), may hold values from -6 to 6
- down_weight: bfloat16 [32, 2880, 2880], P('req', 'hid'), may hold values from -0.0546875 to 0.0546875
- down_bias: bfloat16 [32, 2880], P('req'), may hold values from -6 to 6
Outputs:
- layer_out: bfloat16 [2048, 2880], P('req')
Inputs may be any that keep to these rules, and one draw needn't show every extreme that they name: `routes`: each row names 4 different experts; among the 64 rows of one request group no expert is named by more than 16 rows, and in every draw some expert is named by exactly 16 rows of some group.
All inputs are finite; a program needn't handle non-finite values.
Results may differ from a plain program's by a relative error of at most 0.022.
Values may be sent and summed in bfloat16 or wider, within the bound.
A program may use at most 64 MiB of HBM per device.

v0:
```python
import jax
import jax.numpy as jnp
from jax import lax
from jax.sharding import PartitionSpec as P


def route_tables(routes, experts, capacity):
    row_count, top_count = routes.shape
    pair_ids = routes.reshape(row_count * top_count)
    onehot = (pair_ids[:, None] == jnp.arange(experts, dtype=jnp.int32)[None, :]).astype(jnp.int32)
    before = jnp.cumsum(onehot, axis=0) - onehot
    slot_ids = jnp.sum(before * onehot, axis=1)
    return (pair_ids * capacity + slot_ids).reshape(row_count, top_count)


def placed(target, values, columns_total):
    columns = jnp.arange(columns_total, dtype=jnp.int32)
    matches = target[:, :, None] == columns[None, None, :]
    return jnp.sum(jnp.where(matches, values[:, :, None], 0.0), axis=1)


def on_device(
    attn_partial,
    residual,
    norm_gain,
    router_weight,
    router_bias,
    routes,
    gate_up,
    gate_up_bias,
    down_weight,
    down_bias,
):
    req_count = lax.axis_size("req")
    row_count, features = residual.shape
    experts = router_weight.shape[1]
    top_count = routes.shape[1]
    capacity = 2 * top_count * row_count // req_count
    gain_wide = norm_gain.astype(jnp.float32)
    attention = lax.psum(attn_partial[0].astype(jnp.float32).astype(jnp.bfloat16), "hid").astype(
        jnp.float32
    )
    stream = (residual.astype(jnp.float32) + attention).astype(jnp.bfloat16)
    widened = stream.astype(jnp.float32)
    inverse = lax.rsqrt(jnp.mean(widened * widened, axis=1, keepdims=True) + 1e-05)
    normed = (widened * inverse * gain_wide).astype(jnp.bfloat16)
    logits = jnp.dot(normed, router_weight, preferred_element_type=jnp.float32) + router_bias

    def whole_rows():
        return (normed, widened)

    picked = jnp.take_along_axis(logits, routes, axis=1)
    raised = jnp.exp(picked)
    combine = (raised / jnp.sum(raised, axis=1, keepdims=True)).astype(jnp.bfloat16)
    target = route_tables(routes, experts, capacity)
    slots_total = experts * capacity
    route_matrix = placed(target, jnp.ones(target.shape, jnp.float32), slots_total).astype(
        jnp.bfloat16
    )
    weights_up = gate_up[0]
    normed_full = whole_rows()[0]
    outgoing = jnp.dot(route_matrix.T, normed_full, preferred_element_type=jnp.float32).astype(
        jnp.bfloat16
    )
    outgoing = outgoing.reshape(experts, capacity, features)
    received = lax.all_to_all(outgoing, "req", split_axis=0, concat_axis=0, tiled=True)
    preact = jnp.dot(
        received.reshape(req_count * capacity, features),
        weights_up,
        preferred_element_type=jnp.float32,
    )
    preact = preact + gate_up_bias[0].astype(jnp.float32)
    gate_part = jnp.minimum(preact[:, 0::2], 7.0)
    up_part = jnp.clip(preact[:, 1::2], -7.0, 7.0)
    activated = ((up_part + 1.0) * gate_part * jax.nn.sigmoid(1.702 * gate_part)).astype(
        jnp.bfloat16
    )
    partial_value = jnp.dot(activated, down_weight[0], preferred_element_type=jnp.float32)
    partial_value = partial_value.astype(jnp.bfloat16).astype(jnp.float32)
    combine_matrix = placed(target, combine.astype(jnp.float32), slots_total).astype(jnp.bfloat16)
    summed = lax.psum(partial_value.astype(jnp.bfloat16), "hid").astype(jnp.float32)
    expert_out = (summed + down_bias[0].astype(jnp.float32)).astype(jnp.bfloat16)
    expert_out = expert_out.reshape(req_count, capacity, features)
    returned = lax.all_to_all(expert_out, "req", split_axis=0, concat_axis=0, tiled=True)
    mixture = jnp.dot(
        combine_matrix, returned.reshape(slots_total, features), preferred_element_type=jnp.float32
    )
    widened_full = whole_rows()[1]
    return (widened_full + mixture).astype(jnp.bfloat16)


def solution(mesh):
    return jax.shard_map(
        on_device,
        mesh=mesh,
        in_specs=(
            P("hid", "req", None),
            P("req", None),
            P(),
            P(),
            P(),
            P("req", None),
            P("req", None, "hid"),
            P("req", "hid"),
            P("req", "hid", None),
            P("req", None),
        ),
        out_specs=P("req", None),
        check_vma=False,
    )
```

profile of v0, /device:TPU:1, one launch (start us, length us, event | category | flops | bytes accessed | tf_op | source)
XLA Modules:
  0.0 591.3 jit_solution(12012518058343366653)
XLA Ops:
  6.5 0.0 copy-start
  6.5 0.0 all-reduce.3.cloned.1.call-start
  6.5 0.7 all-reduce.3.cloned.1.call-update
  7.3 0.7 bitcast_or_fusion
  8.0 0.8 copy.39
  8.7 0.1 eq.49
  8.8 0.6 reduce-window.6
  9.4 0.2 slice_reduce_fusion
  9.6 0.1 eq.45
  9.7 0.7 convert_element_type.73
  10.4 0.1 copy.43
  10.5 0.1 reshape.77
  10.7 0.1 fusion.20
  10.8 0.1 reduce_sum.48
  10.9 0.1 copy.42
  11.0 0.7 multiply_add_fusion
  11.7 118.0 %all-reduce.3.cloned.1.call-done = bf16[64,2880]{1,0:T(8,128)(2,1)} async-done(((bf16[64,2880]{1,0:T(8,128)(2,1)}), bf16[64,2880]{1,0:T(8,128)(2,1)}) %all-reduce.3.cloned.1.call-update) | async-done | bytes 368656 | tf_op jit(solution)/shard_map/psum | solution.py:40
  129.7 1.3 fusion.7
  131.0 1.2 convolution_add_fusion.1
  132.3 0.0 copy-start.1
  132.3 2.0 gather_fusion
  134.3 0.1 reshape.80
  134.4 0.1 copy.44
  134.5 0.0 copy-done.1
  134.5 0.2 select_reduce_fusion.1
  134.7 2.7 convolution_convert_fusion.1
  137.4 4.6 copy.45
  142.0 0.0 copy-start.3
  142.0 14.5 %all-to-all-start = ((bf16[32,16,2880]{2,1,0:T(8,128)(2,1)}), bf16[32,16,2880]{2,1,0:T(8,128)(2,1)}, u32[]{:S(2)}, u32[]{:S(2)}) async-start(bf16[32,16,2880]{2,1,0:T(8,128)(2,1)} %bitcast.41), calls=%async_computation | async-start | bytes 6029312 | tf_op jit(solution)/shard_map/all_to_all | solution.py:66
  156.4 0.0 all-reduce.5.cloned.1.call-start
  156.5 0.0 copy-done.3
  156.5 135.6 %all-to-all-done = bf16[32,16,2880]{2,1,0:T(8,128)(2,1)} async-done(((bf16[32,16,2880]{2,1,0:T(8,128)(2,1)}), bf16[32,16,2880]{2,1,0:T(8,128)(2,1)}, u32[]{:S(2)}, u32[]{:S(2)}) %all-to-all-start) | async-done | bytes 2949152 | tf_op jit(solution)/shard_map/all_to_all | solution.py:66
  292.2 0.0 copy-done
  292.2 3.2 fusion.3
  295.4 1.5 slice.14
  296.8 1.4 slice.15
  298.3 4.2 convolution_convert_fusion
  302.5 0.0 copy-start.2
  302.5 0.0 all-reduce.5.cloned.1.call-update
  302.5 0.7 copy-done.2
  303.2 117.7 %all-reduce.5.cloned.1.call-done = bf16[512,2880]{0,1:T(8,128)(2,1)} async-done(((bf16[512,2880]{0,1:T(8,128)(2,1)}), bf16[512,2880]{0,1:T(8,128)(2,1)}) %all-reduce.5.cloned.1.call-update) | async-done | bytes 2949136 | tf_op jit(solution)/shard_map/psum | solution.py:81
  420.9 4.1 add_convert_fusion
  425.0 4.6 copy.46
  429.5 153.5 %all_to_all.10 = bf16[32,16,2880]{2,1,0:T(8,128)(2,1)S(1)} all-to-all(bf16[32,16,2880]{2,1,0:T(8,128)(2,1)} %bitcast.42), channel_id=1, replica_groups=mesh['req'=32,'hid'=16] {'req'}, dimensions={0} | all-to-all | bytes 5898240 | tf_op jit(solution)/shard_map/all_to_all | solution.py:84
  583.0 1.4 fusion
  (8 shorter events, 0.2 us)
Async XLA Ops:
  6.5 285.6 %copy-start = (bf16[1,2880,360]{1,2,0:T(8,128)(2,1)S(1)}, bf16[1,2880,360]{1,2,0:T(8,128)(2,1)}, u32[]{:S(2)}) copy-start(bf16[1,2880,360]{1,2,0:T(8,128)(2,1)} %param.16) | copy-start | bytes 6220804
  6.5 123.1 %all-reduce.3.cloned.1.call-start = ((), (), s32[]{:S(2)}) async-start(), calls=%async_computation.2 | async-start | bytes 753664 | tf_op jit(solution)/shard_map/psum | solution.py:40
  132.3 2.2 copy-start.1
  142.0 14.5 %copy-start.3 = (bf16[1,360]{1,0:T(2,128)(2,1)S(1)}, bf16[1,360]{1,0:T(2,128)(2,1)}, u32[]{:S(2)}) copy-start(bf16[1,360]{1,0:T(2,128)(2,1)} %param.17) | copy-start | bytes 2164
  142.0 150.2 %all-to-all-start = ((bf16[32,16,2880]{2,1,0:T(8,128)(2,1)}), bf16[32,16,2880]{2,1,0:T(8,128)(2,1)}, u32[]{:S(2)}, u32[]{:S(2)}) async-start(bf16[32,16,2880]{2,1,0:T(8,128)(2,1)} %bitcast.41), calls=%async_computation | async-start | bytes 6029312 | tf_op jit(solution)/shard_map/all_to_all | solution.py:66
  156.4 264.5 %all-reduce.5.cloned.1.call-start = ((), (), s32[]{:S(2)}) async-start(), calls=%async_computation.3 | async-start | bytes 5898240 | tf_op jit(solution)/shard_map/psum | solution.py:81
  302.5 0.7 copy-start.2
Sparse Core Ops, SparseCore 0:
  10.6 119.0 all-reduce.2
  302.6 118.2 all-reduce.4
where the time goes:
time: 592 us; the launch traced here: 591 us
  waiting for transfers between devices  372 us (63%)
  blocking collectives  154 us (26%)
  local copies, waits for them, and re-layouts  16.5 us (3%)
  starting transfers between devices  14.5 us (2%)
  between operations  13.5 us (2%)
  matrix products  12.7 us (2%)
  other arithmetic  8.49 us (1%)
    all_to_all x1, blocking collectives, on_device(): lax.all_to_all(expert_out, 'req', split_axis=0, concat_axis=0, tiled=True)  154 us
    all_to_all x1, waiting for transfers between devices, on_device(): lax.all_to_all(outgoing, 'req', split_axis=0, concat_axis=0, tiled=True)  136 us
    psum x1, waiting for transfers between devices, on_device(): lax.psum(attn_partial[0].astype(jnp.float32).astype(jnp.bfloat16), 'hid')  118 us
    psum x1, waiting for transfers between devices, on_device(): lax.psum(partial_value.astype(jnp.bfloat16), 'hid').astype(jnp.float32)  118 us
    all_to_all x1, starting transfers between devices, on_device(): lax.all_to_all(outgoing, 'req', split_axis=0, concat_axis=0, tiled=True)  14.5 us
  transfers between devices with their start and end apart: 3, of which 3 were waited for; matrix products, arithmetic and copies ran while one was open for 1% of the time, Pallas kernels for 0%

commit v1 on v0

--- a/solution.py
+++ b/solution.py
@@ -37,9 +37,9 @@
     top_count = routes.shape[1]
     capacity = 2 * top_count * row_count // req_count
     gain_wide = norm_gain.astype(jnp.float32)
-    attention = lax.psum(attn_partial[0].astype(jnp.float32).astype(jnp.bfloat16), "hid").astype(
-        jnp.float32
-    )
+    attention = jnp.sum(
+        lax.all_gather(attn_partial[0].astype(jnp.float32).astype(jnp.bfloat16), "hid"), axis=0
+    ).astype(jnp.float32)
     stream = (residual.astype(jnp.float32) + attention).astype(jnp.bfloat16)
     widened = stream.astype(jnp.float32)
     inverse = lax.rsqrt(jnp.mean(widened * widened, axis=1, keepdims=True) + 1e-05)

time: 592 us -> 554 us (0.936)
  waiting for transfers between devices: 372 us -> 335 us
    psum x1 -> x0, waiting for transfers between devices: 118 us -> none  [on_device(): lax.psum(attn_partial[0].astype(jnp.float32).astype(jnp.bfloat16), 'hid')]
    all_gather x0 -> x1, waiting for transfers between devices: none -> 79.5 us  [on_device(): lax.all_gather(attn_partial[0].astype(jnp.float32).astype(jnp.bfloat16),...]
where the time goes in v1:
time: 554 us; the launch traced here: 553 us
  waiting for transfers between devices  335 us (60%)
  blocking collectives  154 us (28%)
  local copies, waits for them, and re-layouts  15.8 us (3%)
  between operations  13.6 us (2%)
  starting transfers between devices  13.2 us (2%)
  matrix products  11.8 us (2%)
  other arithmetic  11 us (2%)
    all_to_all x1, blocking collectives, on_device(): lax.all_to_all(expert_out, 'req', split_axis=0, concat_axis=0, tiled=True)  154 us
    all_to_all x1, waiting for transfers between devices, on_device(): lax.all_to_all(outgoing, 'req', split_axis=0, concat_axis=0, tiled=True)  136 us
    psum x1, waiting for transfers between devices, on_device(): lax.psum(partial_value.astype(jnp.bfloat16), 'hid').astype(jnp.float32)  119 us
    all_gather x1, waiting for transfers between devices, on_device(): lax.all_gather(attn_partial[0].astype(jnp.float32).astype(jnp.bfloat16),...  79.5 us
    all_to_all x1, starting transfers between devices, on_device(): lax.all_to_all(outgoing, 'req', split_axis=0, concat_axis=0, tiled=True)  13.2 us
  transfers between devices with their start and end apart: 3, of which 3 were waited for; matrix products, arithmetic and copies ran while one was open for 1% of the time, Pallas kernels for 0%

profile of v1, /device:TPU:1, one launch (start us, length us, event | category | flops | bytes accessed | tf_op | source)
XLA Modules:
  0.0 553.5 jit_solution(728477529178288856)
XLA Ops:
  6.5 0.0 copy-start
  6.5 0.0 all-gather.2.cloned.1.call-start
  6.5 0.7 all-gather.2.cloned.1.call-update
  7.3 0.8 copy.51
  8.0 0.1 eq.49
  8.1 0.1 eq.45
  8.2 0.7 convert_element_type.75
  8.9 0.7 bitcast_or_fusion
  9.6 0.1 copy.55
  9.7 0.1 reshape.78
  9.9 0.6 reduce-window.6
  10.4 0.2 slice_reduce_fusion
  10.7 0.1 fusion.20
  10.8 0.1 reduce_sum.61
  10.9 0.1 copy.54
  11.0 0.7 multiply_add_fusion
  11.7 0.0 copy-start.1
  11.7 79.5 %all-gather.2.cloned.1.call-done = bf16[16,64,2880]{2,1,0:T(8,128)(2,1)} async-done(((bf16[1,64,2880]{2,1,0:T(8,128)(2,1)}), bf16[16,64,2880]{2,1,0:T(8,128)(2,1)}) %all-gather.2.cloned.1.call-update) | async-done | bytes 5898256 | tf_op jit(solution)/shard_map/all_gather | solution.py:41
  91.2 3.6 reduce_sum.59
  94.8 0.0 copy-done.1
  94.8 0.2 fusion.7
  95.1 0.0 copy-done.5
  95.1 0.0 copy-done.6
  95.1 0.3 convolution_add_fusion.1
  95.4 0.0 copy-start.2
  95.4 2.0 gather_fusion
  97.4 0.1 reshape.81
  97.5 0.1 copy.56
  97.6 0.0 copy-done.2
  97.6 0.2 select_reduce_fusion.1
  97.8 2.7 convolution_convert_fusion.1
  100.5 4.6 copy.57
  105.1 13.2 %all-to-all-start = ((bf16[32,16,2880]{2,1,0:T(8,128)(2,1)}), bf16[32,16,2880]{2,1,0:T(8,128)(2,1)}, u32[]{:S(2)}, u32[]{:S(2)}) async-start(bf16[32,16,2880]{2,1,0:T(8,128)(2,1)} %bitcast.40), calls=%async_computation | async-start | bytes 6029312 | tf_op jit(solution)/shard_map/all_to_all | solution.py:66
  118.3 0.0 all-reduce.2.cloned.1.call-start
  118.3 0.0 copy-done.4
  118.4 135.6 %all-to-all-done = bf16[32,16,2880]{2,1,0:T(8,128)(2,1)} async-done(((bf16[32,16,2880]{2,1,0:T(8,128)(2,1)}), bf16[32,16,2880]{2,1,0:T(8,128)(2,1)}, u32[]{:S(2)}, u32[]{:S(2)}) %all-to-all-start) | async-done | bytes 2949152 | tf_op jit(solution)/shard_map/all_to_all | solution.py:66
  254.0 0.0 copy-done
  254.0 3.2 fusion.3
  257.2 1.5 slice.14
  258.6 1.4 slice.15
  260.1 4.2 convolution_convert_fusion
  264.3 0.0 all-reduce.2.cloned.1.call-update
  264.3 0.0 copy-done.3
  264.4 118.7 %all-reduce.2.cloned.1.call-done = bf16[512,2880]{0,1:T(8,128)(2,1)} async-done(((bf16[512,2880]{0,1:T(8,128)(2,1)}), bf16[512,2880]{0,1:T(8,128)(2,1)}) %all-reduce.2.cloned.1.call-update) | async-done | bytes 2949136 | tf_op jit(solution)/shard_map/psum | solution.py:81
  383.1 4.1 add_convert_fusion
  387.1 4.6 copy.58
  391.7 153.5 %all_to_all.10 = bf16[32,16,2880]{2,1,0:T(8,128)(2,1)S(1)} all-to-all(bf16[32,16,2880]{2,1,0:T(8,128)(2,1)} %bitcast.41), channel_id=1, replica_groups=mesh['req'=32,'hid'=16] {'req'}, dimensions={0} | all-to-all | bytes 5898240 | tf_op jit(solution)/shard_map/all_to_all | solution.py:84
  545.2 1.4 fusion
  (12 shorter events, 0.2 us)
Async XLA Ops:
  6.5 247.5 %copy-start = (bf16[1,2880,360]{1,2,0:T(8,128)(2,1)S(1)}, bf16[1,2880,360]{1,2,0:T(8,128)(2,1)}, u32[]{:S(2)}) copy-start(bf16[1,2880,360]{1,2,0:T(8,128)(2,1)} %param.16) | copy-start | bytes 6220804
  6.5 84.6 %all-gather.2.cloned.1.call-start = ((), (), s32[]{:S(2)}) async-start(), calls=%async_computation.2 | async-start | bytes 6406144 | tf_op jit(solution)/shard_map/all_gather | solution.py:41
  11.7 83.1 %copy-start.1 = (bf16[64,2880]{1,0:T(8,128)(2,1)S(1)}, bf16[64,2880]{1,0:T(8,128)(2,1)}, u32[]{:S(2)}) copy-start(bf16[64,2880]{1,0:T(8,128)(2,1)} %param.11) | copy-start | bytes 1105924
  11.7 83.4 %copy-start.5 = (bf16[2880,32]{0,1:T(8,128)(2,1)S(1)}, bf16[2880,32]{0,1:T(8,128)(2,1)}, u32[]{:S(2)}) copy-start(bf16[2880,32]{0,1:T(8,128)(2,1)} %param.13) | copy-start | bytes 552964
  11.7 83.4 %copy-start.6 = (f32[32]{0:T(128)S(1)}, f32[32]{0:T(128)}, u32[]{:S(2)}) copy-start(f32[32]{0:T(128)} %param.14) | copy-start | bytes 388
  95.4 2.2 copy-start.2
  105.1 13.3 %copy-start.4 = (bf16[1,360]{1,0:T(2,128)(2,1)S(1)}, bf16[1,360]{1,0:T(2,128)(2,1)}, u32[]{:S(2)}) copy-start(bf16[1,360]{1,0:T(2,128)(2,1)} %param.17) | copy-start | bytes 2164
  105.1 148.9 %all-to-all-start = ((bf16[32,16,2880]{2,1,0:T(8,128)(2,1)}), bf16[32,16,2880]{2,1,0:T(8,128)(2,1)}, u32[]{:S(2)}, u32[]{:S(2)}) async-start(bf16[32,16,2880]{2,1,0:T(8,128)(2,1)} %bitcast.40), calls=%async_computation | async-start | bytes 6029312 | tf_op jit(solution)/shard_map/all_to_all | solution.py:66
  118.3 264.8 %all-reduce.2.cloned.1.call-start = ((), (), s32[]{:S(2)}) async-start(), calls=%async_computation.3 | async-start | bytes 5898240 | tf_op jit(solution)/shard_map/psum | solution.py:81
  260.1 4.2 copy-start.3
Sparse Core Ops, SparseCore 0:
  10.4 80.7 all-gather.1
  264.4 118.5 all-reduce.1
